TPU v7x, 256 devices: a whole 4x4x8 slice. The times are simulated.
256 devices in a mesh: seq: 32 (over y, x, core), grp: 8 (over z).
Axes of the slice: x: 4, y: 4, z: 8, core: 2. Of those that a mesh axis runs over, the one named last changes fastest.
Arguments:
- hidden_in: bfloat16 [98304, 2048], P(('grp', 'seq')), parts along dimension 0, may hold values from -8 to 8
- norm_gain: bfloat16 [2048], replicated, may hold values from 0.099609375 to 1.8984375
- w_query: bfloat16 [2048, 2048], P('seq'), may hold values from -1 to 1
- w_key: bfloat16 [2048, 128], P('seq'), may hold values from -1 to 1
- w_value: bfloat16 [2048, 128], P('seq'), may hold values from -0.125 to 0.125
- w_out: bfloat16 [2048, 2048], P('seq'), may hold values from -0.625 to 0.625
- seg_ids: int32 [98304], P('grp'), parts along dimension 0, may hold values from 0 to 1, never falling along the last dimension, each value on 1 to 11904 neighbouring positions
- cache_slot: int32 [768], P('grp'), parts along dimension 0, may hold values from 0 to 95, each once
Outputs:
- hidden_out: bfloat16 [98304, 2048], P(('grp', 'seq')), parts along dimension 0
- kv_cache: bfloat16 [98304, 256], P(('grp', 'seq')), parts along dimension 0
There are 8 independent parts, one for each index of `grp`. A program takes and returns all parts, laid end to end along the dimension named above; an argument that names none is the same for every part. Nothing has to cross between parts.
Inputs may be any that keep to these rules, and one draw needn't show every extreme that they name: `seg_ids`: segment numbers never fall along the stream; each prompt holds 1 to 11904 tokens. `cache_slot`: every cache position appears exactly once.
All inputs are finite; a program needn't handle non-finite values.
Results may differ from a plain program's by a relative error of at most 0.01.
Values may be sent and summed in bfloat16 or wider, within the bound.
No kernel may reach another device: no remote copies, remote signals or barrier semaphores. Data moves between devices by JAX's collectives and lax.ppermute only.
A program may use at most 256 MiB of HBM per device.

v0:
```python
import jax
import jax.numpy as jnp
from jax import lax
from jax.sharding import PartitionSpec as P

WINDOW = 1024
CACHE_BLK = 128
REACH = 3
EPSILON = 1e-06


def shifted(array, axis, by):
    length = lax.axis_size(axis)
    pairs = [(i, i + by) for i in range(length) if 0 <= i + by < length]
    return lax.ppermute(array, axis, pairs)


def normalize(hidden_in, norm_gain):
    values_wide = hidden_in.astype(jnp.float32)
    mean_square = jnp.mean(values_wide * values_wide, axis=1, keepdims=True)
    return (values_wide * lax.rsqrt(mean_square + EPSILON) * norm_gain.astype(jnp.float32)).astype(
        jnp.bfloat16
    )


def attend_block(queries, key_rows, value_rows, seg_query, seg_key, pos_query, pos_key):
    row_count = queries.shape[0]
    head_dim = key_rows.shape[1]
    head_count = queries.shape[1] // head_dim
    visible = (
        (seg_query[:, None] == seg_key[None, :])
        & (pos_key[None, :] <= pos_query[:, None])
        & (pos_key[None, :] > pos_query[:, None] - WINDOW)
    )
    score_scale = 1.0 / head_dim**0.5

    def one_head(query_head):
        scores = (
            lax.dot_general(
                query_head, key_rows, (((1,), (1,)), ((), ())), preferred_element_type=jnp.float32
            )
            * score_scale
        )
        scores = jnp.where(visible, scores, -jnp.inf)
        row_top = jnp.max(scores, axis=1, keepdims=True)
        weights = jnp.exp(scores - row_top).astype(jnp.bfloat16)
        weight_sum = jnp.sum(weights.astype(jnp.float32), axis=1, keepdims=True)
        mixture = jnp.dot(weights, value_rows, preferred_element_type=jnp.float32) / weight_sum
        return mixture.astype(jnp.bfloat16)

    per_head = jnp.transpose(queries.reshape(row_count, head_count, head_dim), (1, 0, 2))
    result = lax.map(one_head, per_head)
    return jnp.transpose(result, (1, 0, 2)).reshape(row_count, head_count * head_dim)


def shards(hidden_in, norm_gain, w_query, w_key, w_value, w_out, seg_ids, cache_slot):
    row_count = hidden_in.shape[0]
    devices = lax.axis_size("seq")
    my_index = lax.axis_index("seq")
    normed = normalize(hidden_in, norm_gain)
    head_dim = w_key.shape[1]
    pieces = (
        lax.all_gather(w_query, "seq", axis=0, tiled=True),
        lax.all_gather(w_key, "seq", axis=0, tiled=True),
        lax.all_gather(w_value, "seq", axis=0, tiled=True),
    )
    columns = normed
    query_sum, key_sum, value_sum = tuple(
        (jnp.dot(columns, piece, preferred_element_type=jnp.float32) for piece in pieces)
    )
    query = query_sum.astype(jnp.bfloat16)
    stacked = jnp.concatenate(
        [key_sum.astype(jnp.bfloat16), value_sum.astype(jnp.bfloat16)], axis=1
    )
    margin = REACH * row_count
    span = (REACH + 1) * row_count
    reach_now = min(REACH, devices - 1)
    missing = jnp.zeros(((REACH - reach_now) * row_count, 2 * head_dim), jnp.bfloat16)
    received = []
    current = stacked
    for distance in range(reach_now):
        current = shifted(current, "seq", 1)
        received.append(current)
    window_rows = jnp.concatenate([missing] + received[::-1] + [stacked], axis=0)
    first_row = my_index * row_count
    seg_pad = jnp.concatenate([jnp.full((margin,), -1, jnp.int32), seg_ids])
    seg_query = lax.dynamic_slice_in_dim(seg_ids, first_row, row_count, 0)
    seg_key = lax.dynamic_slice_in_dim(seg_pad, first_row, span, 0)
    pos_query = first_row + jnp.arange(row_count, dtype=jnp.int32)
    pos_key = first_row - margin + jnp.arange(span, dtype=jnp.int32)
    attended = attend_block(
        query,
        window_rows[:, :head_dim],
        window_rows[:, head_dim:],
        seg_query,
        seg_key,
        pos_query,
        pos_key,
    )
    columns = attended
    projected = jnp.dot(
        columns,
        lax.all_gather(w_out, "seq", axis=0, tiled=True),
        preferred_element_type=jnp.float32,
    )
    hidden_out = (hidden_in.astype(jnp.float32) + projected).astype(jnp.bfloat16)
    blocks_per_dev = row_count // CACHE_BLK
    block_total = cache_slot.shape[0]
    slot_ids = jnp.arange(block_total, dtype=jnp.int32)
    source_of = jnp.sum(
        jnp.where(cache_slot[None, :] == slot_ids[:, None], slot_ids[None, :], 0), axis=1
    )
    owned_sources = lax.dynamic_slice_in_dim(
        source_of, my_index * blocks_per_dev, blocks_per_dev, 0
    )
    within = jnp.arange(row_count, dtype=jnp.int32)
    source_row = (
        jnp.repeat(owned_sources, CACHE_BLK, total_repeat_length=row_count) * CACHE_BLK
        + within % CACHE_BLK
    )
    piece = lax.all_gather(stacked, "seq", axis=0, tiled=True)
    inside = (source_row >= 0) & (source_row < piece.shape[0])
    taken = jnp.take(piece, jnp.clip(source_row, 0, piece.shape[0] - 1), axis=0)
    kv_cache = jnp.where(inside[:, None], taken, jnp.zeros_like(stacked))
    return (hidden_out, kv_cache)


def solution(mesh):
    in_specs = (
        P(("grp", "seq"), None),
        P(),
        P("seq", None),
        P("seq", None),
        P("seq", None),
        P("seq", None),
        P("grp"),
        P("grp"),
    )
    out_specs = (P(("grp", "seq"), None), P(("grp", "seq"), None))
    return jax.shard_map(shards, mesh=mesh, in_specs=in_specs, out_specs=out_specs, check_vma=False)
```

profile of v0, /device:TPU:1, one launch (start us, length us, event | category | flops | bytes accessed | tf_op | source)
XLA Modules:
  0.0 271.4 jit_solution(2322478954140555485)
XLA Ops:
  7.2 0.8 convert_element_type.32
  8.0 1.8 fusion.8
  9.8 26.4 %all_gather.17 = bf16[2048,128]{1,0:T(8,128)(2,1)S(1)} all-gather(bf16[64,128]{1,0:T(8,128)(2,1)} %param.16), channel_id=1, replica_groups=mesh['seq'=32,'grp'=8] {'seq'}, dimensions={0}, use_global_device_ids=true | all-gather | bytes 540672 | tf_op jit(solution)/shard_map/all_gather | solution.py:65
  36.3 24.1 %all_gather.16 = bf16[2048,128]{1,0:T(8,128)(2,1)S(1)} all-gather(bf16[64,128]{1,0:T(8,128)(2,1)} %param.15), channel_id=1, replica_groups=mesh['seq'=32,'grp'=8] {'seq'}, dimensions={0}, use_global_device_ids=true | all-gather | bytes 540672 | tf_op jit(solution)/shard_map/all_gather | solution.py:64
  60.4 0.7 convolution_convert_fusion.1
  61.1 0.7 convolution_convert_fusion.2
  61.9 0.7 pad_maximum_fusion
  62.6 0.7 all-gather.4.cloned.1.call-update
  63.4 1.9 collective-permute-start
  65.6 0.7 fusion.30
  66.3 2.0 fusion.23
  68.4 4.1 %collective-permute-start.1 = (bf16[384,256]{0,1:T(8,128)(2,1)S(1)}, bf16[384,256]{0,1:T(8,128)(2,1)S(1)}, u32[]{:S(2)}, u32[]{:S(2)}) collective-permute-start(bf16[384,256]{0,1:T(8,128)(2,1)S(1)} %collective-permute-done), channel_id=1, source_target_pairs={{0,8},{8,16},{16,24},{24,32},{32,40},{40,48},{48,56},{56,64},{64,7... | collective-permute-start | bytes 589832 | tf_op jit(solution)/shard_map/ppermute | solution.py:15
  72.5 2.6 collective-permute-done.1
  75.1 4.6 %collective-permute-start.2 = (bf16[384,256]{0,1:T(8,128)(2,1)S(1)}, bf16[384,256]{0,1:T(8,128)(2,1)S(1)}, u32[]{:S(2)}, u32[]{:S(2)}) collective-permute-start(bf16[384,256]{0,1:T(8,128)(2,1)S(1)} %collective-permute-done.1), channel_id=1, source_target_pairs={{0,8},{8,16},{16,24},{24,32},{32,40},{40,48},{48,56},{56,64},{64,7... | collective-permute-start | bytes 589832 | tf_op jit(solution)/shard_map/ppermute | solution.py:15
  79.7 3.3 %collective-permute-done.2 = bf16[384,256]{0,1:T(8,128)(2,1)S(1)} collective-permute-done((bf16[384,256]{0,1:T(8,128)(2,1)S(1)}, bf16[384,256]{0,1:T(8,128)(2,1)S(1)}, u32[]{:S(2)}, u32[]{:S(2)}) %collective-permute-start.2) | collective-permute-done | bytes 196640 | tf_op jit(solution)/shard_map/ppermute | solution.py:15
  83.1 0.9 copy.20
  84.0 0.9 copy.21
  84.9 37.7 %all-gather.8.cloned.1.call-done = bf16[12288,256]{0,1:T(8,128)(2,1)} async-done(((bf16[384,256]{0,1:T(8,128)(2,1)}), bf16[12288,256]{0,1:T(8,128)(2,1)}) %all-gather.8.cloned.1.call-update) | async-done | bytes 6291472 | tf_op jit(solution)/shard_map/all_gather | solution.py:121
  122.7 8.6 %copy.23 = bf16[12288,256]{1,0:T(8,128)(2,1)} copy(bf16[12288,256]{0,1:T(8,128)(2,1)} %all-gather.8.cloned.1.call-done) | data formatting | bytes 12582912 | tf_op jit(solution)/shard_map/all_gather | solution.py:121
  131.3 5.3 %gather_fusion = bf16[384,256]{1,0:T(8,128)(2,1)S(1)} fusion(bf16[12288,256]{1,0:T(8,128)(2,1)} %copy.23, s32[1024]{0:T(1024)S(1)} %pad_clamp_fusion), kind=kCustom, calls=%fused_computation | custom fusion | bytes 394752 | tf_op jit(solution)/shard_map/jit(_take)/gather | solution.py:123
  136.6 0.8 select_select_fusion
  137.4 45.4 %all-gather.4.cloned.1.call-done = bf16[2048,2048]{1,0:T(8,128)(2,1)} async-done(((bf16[64,2048]{1,0:T(8,128)(2,1)}), bf16[2048,2048]{1,0:T(8,128)(2,1)}) %all-gather.4.cloned.1.call-update) | async-done | bytes 8388624 | tf_op jit(solution)/shard_map/all_gather | solution.py:63
  182.8 6.8 %fusion.12 = bf16[48,16,8,128]{3,2,1,0:T(8,128)(2,1)S(1)} fusion(bf16[2048,2048]{1,0:T(8,128)(2,1)} %all-gather.4.cloned.1.call-done, bf16[384,2048]{1,0:T(8,128)(2,1)S(1)} %copy-done, f32[2048]{0:T(1024)S(1)} %convert_element_type.32, f32[384]{0:T(512)S(1)} %add_rsqrt_fusion), kind=kOutput, calls=%fused_computation.22 | convolution fusion | flops 3225157632 | bytes 11544064 | tf_op jit(solution)/shard_map/dot_general | solution.py:69
  190.1 66.2 %while.12 = (s32[]{:T(128)}, bf16[16,384,128]{1,2,0:T(8,128)(2,1)}, bf16[16,384,128]{2,1,0:T(8,128)(2,1)S(1)}, bf16[1536,128]{1,0:T(8,128)(2,1)}, bf16[1536,128]...) while((s32[]{:T(128)}, bf16[16,384,128]{1,2,0:T(8,128)(2,1)}, ...), condition=%wide.region_4.5_spmd.clone, body=%wide.region_1.4_spmd.clone.sunk | while | flops 309165312 | bytes 10055833 | solution.py:52
  190.1 1.9 fusion.47
  194.2 1.9 fusion.47
  198.4 1.9 fusion.47
  201.8 0.7 constant_dynamic-update-slice_fusion.2
  202.5 1.9 fusion.47
  206.0 0.7 constant_dynamic-update-slice_fusion.2
  206.6 1.9 fusion.47
  210.1 0.7 constant_dynamic-update-slice_fusion.2
  210.8 1.9 fusion.47
  214.9 1.9 fusion.47
  219.0 1.9 fusion.47
  222.5 0.7 constant_dynamic-update-slice_fusion.2
  223.2 1.9 fusion.47
  227.3 1.9 fusion.47
  230.8 0.7 constant_dynamic-update-slice_fusion.2
  231.5 1.9 fusion.47
  235.6 1.9 fusion.47
  239.1 0.7 constant_dynamic-update-slice_fusion.2
  239.8 1.9 fusion.47
  244.0 1.9 fusion.47
  248.1 1.9 fusion.47
  252.2 1.9 fusion.47
  255.7 0.7 constant_dynamic-update-slice_fusion.2
  256.3 8.5 %fusion.11 = bf16[384,2048]{1,0:T(8,128)(2,1)} fusion(bf16[384,2048]{1,0:T(8,128)(2,1)S(1)} %copy-done, bf16[384,2048]{0,1:T(8,128)(2,1)} %bitcast.62, bf16[2048,2048]{1,0:T(8,128)(2,1)} %all-gather.6.cloned.1.call-done), kind=kOutput, calls=%fused_computation.19 | convolution fusion | flops 3223584768 | bytes 13107200 | tf_op jit(solution)/shard_map/dot_general | solution.py:101
  (116 shorter events, 32.4 us)
Async XLA Ops:
  7.2 53.2 %copy-start = (bf16[384,2048]{1,0:T(8,128)(2,1)S(1)}, bf16[384,2048]{1,0:T(8,128)(2,1)}, u32[]{:S(2)}) copy-start(bf16[384,2048]{1,0:T(8,128)(2,1)} %param.12) | copy-start | bytes 4718596
  7.2 115.5 %all-gather.8.cloned.1.call-start = ((), (), s32[]{:S(2)}) async-start(), calls=%async_computation.2 | async-start | bytes 6488064 | tf_op jit(solution)/shard_map/all_gather | solution.py:121
  61.1 4.3 %copy-start.3 = (s32[96]{0:T(128)S(1)}, s32[96]{0:T(128)}, u32[]{:S(2)}) copy-start(s32[96]{0:T(128)} %param.19) | copy-start | bytes 1156
  61.1 5.1 %copy-start.2 = (s32[12288]{0:T(1024)S(1)}, s32[12288]{0:T(1024)}, u32[]{:S(2)}) copy-start(s32[12288]{0:T(1024)} %param.18) | copy-start | bytes 147460
  62.6 120.3 %all-gather.4.cloned.1.call-start = ((), (), s32[]{:S(2)}) async-start(), calls=%async_computation | async-start | bytes 8650752 | tf_op jit(solution)/shard_map/all_gather | solution.py:63
  63.3 193.0 %all-gather.6.cloned.1.call-start = ((), (), s32[]{:S(2)}) async-start(), calls=%async_computation.1 | async-start | bytes 8650752 | tf_op jit(solution)/shard_map/all_gather | solution.py:103
  63.4 5.0 %collective-permute-start = (bf16[384,256]{0,1:T(8,128)(2,1)}, bf16[384,256]{0,1:T(8,128)(2,1)S(1)}, u32[]{:S(2)}, u32[]{:S(2)}) collective-permute-start(bf16[384,256]{0,1:T(8,128)(2,1)} %pad_maximum_fusion), channel_id=1, source_target_pairs={{0,8},{8,16},{16,24},{24,32},{32,40},{40,48},{48,56},{56,64},{64,7... | collective-permute-start | bytes 589832 | tf_op jit(solution)/shard_map/ppermute | solution.py:15
  68.4 6.7 %collective-permute-start.1 = (bf16[384,256]{0,1:T(8,128)(2,1)S(1)}, bf16[384,256]{0,1:T(8,128)(2,1)S(1)}, u32[]{:S(2)}, u32[]{:S(2)}) collective-permute-start(bf16[384,256]{0,1:T(8,128)(2,1)S(1)} %collective-permute-done), channel_id=1, source_target_pairs={{0,8},{8,16},{16,24},{24,32},{32,40},{40,48},{48,56},{56,64},{64,7... | collective-permute-start | bytes 589832 | tf_op jit(solution)/shard_map/ppermute | solution.py:15
  75.1 7.9 %collective-permute-start.2 = (bf16[384,256]{0,1:T(8,128)(2,1)S(1)}, bf16[384,256]{0,1:T(8,128)(2,1)S(1)}, u32[]{:S(2)}, u32[]{:S(2)}) collective-permute-start(bf16[384,256]{0,1:T(8,128)(2,1)S(1)} %collective-permute-done.1), channel_id=1, source_target_pairs={{0,8},{8,16},{16,24},{24,32},{32,40},{40,48},{48,56},{56,64},{64,7... | collective-permute-start | bytes 589832 | tf_op jit(solution)/shard_map/ppermute | solution.py:15
  192.0 1.0 copy-start.1
  196.1 1.0 copy-start.1
  200.2 1.0 copy-start.1
  204.4 1.0 copy-start.1
  208.5 1.0 copy-start.1
  212.6 1.0 copy-start.1
  216.7 1.0 copy-start.1
  220.9 1.0 copy-start.1
  225.1 1.0 copy-start.1
  229.2 1.0 copy-start.1
  233.4 1.0 copy-start.1
  237.5 1.0 copy-start.1
  241.7 1.0 copy-start.1
  245.8 1.0 copy-start.1
  249.9 1.0 copy-start.1
  254.1 1.0 copy-start.1
Sparse Core Ops, SparseCore 0:
  62.7 59.9 all-gather.7
  125.2 57.5 all-gather.3
  185.4 57.5 all-gather.5
where the time goes:
time: 273 us; the launch traced here: 271 us
  waiting for transfers between devices  89.7 us (33%)
  matrix products  54.3 us (20%)
  blocking collectives  50.5 us (18%)
  local copies, waits for them, and re-layouts  37.7 us (14%)
  other arithmetic  14.3 us (5%)
  between operations  13.9 us (5%)
  starting transfers between devices  10.7 us (4%)
    all_gather x1, waiting for transfers between devices, shards(): lax.all_gather(w_query, 'seq', axis=0, tiled=True)  45.4 us
    all_gather x1, waiting for transfers between devices, shards(): piece = lax.all_gather(stacked, 'seq', axis=0, tiled=True)  37.7 us
    dot_general x16, matrix products, one_head(): lax.dot_general(query_head, key_rows, (((1,), (1,)), ((), ())), preferred...  30 us
    all_gather x1, blocking collectives, shards(): lax.all_gather(w_value, 'seq', axis=0, tiled=True)  26.4 us
    all_gather x1, blocking collectives, shards(): lax.all_gather(w_key, 'seq', axis=0, tiled=True)  24.1 us
    dynamic_update_slice x32, local copies, waits for them, and re-layouts, attend_block(): result = lax.map(one_head, per_head)  12.5 us
    ppermute x3, starting transfers between devices, shifted(): return lax.ppermute(array, axis, pairs)  10.5 us
    all_gather x1, local copies, waits for them, and re-layouts, shards(): piece = lax.all_gather(stacked, 'seq', axis=0, tiled=True)  8.63 us
  transfers between devices with their start and end apart: 6, of which 4 were waited for; matrix products, arithmetic and copies ran while one was open for 31% of the time, Pallas kernels for 0%

commit v1 on v0

--- a/solution.py
+++ b/solution.py
@@ -62,7 +62,9 @@
     pieces = (
         lax.all_gather(w_query, "seq", axis=0, tiled=True),
         lax.all_gather(w_key, "seq", axis=0, tiled=True),
-        lax.all_gather(w_value, "seq", axis=0, tiled=True),
+        jnp.concatenate(
+            lax.all_to_all(jnp.stack([w_value] * lax.axis_size("seq")), "seq", 0, 0), axis=0
+        ),
     )
     columns = normed
     query_sum, key_sum, value_sum = tuple(

time: 273 us -> 258 us (0.945)
  blocking collectives: 50.5 us -> 27.6 us
  starting transfers between devices: 10.7 us -> 19.5 us
    all_gather x1 -> x0, blocking collectives: 26.4 us -> none  [shards(): lax.all_gather(w_value, 'seq', axis=0, tiled=True)]
    all_to_all x0 -> x1, starting transfers between devices: none -> 8.59 us  [shards(): lax.all_to_all(jnp.stack([w_value] * lax.axis_size('seq')), 'seq', 0, 0)]
    all_gather x1, waiting for transfers between devices: 37.7 us -> 33.3 us  [shards(): piece = lax.all_gather(stacked, 'seq', axis=0, tiled=True)]
    ppermute x3, waiting for transfers between devices: 5.86 us -> 9.39 us  [shifted(): return lax.ppermute(array, axis, pairs)]
    all_gather x1, blocking collectives: 24.1 us -> 27.6 us  [shards(): lax.all_gather(w_key, 'seq', axis=0, tiled=True)]
  transfers between devices with their start and end apart: 6 -> 7, of which waited for: 4 -> 5; matrix products, arithmetic and copies ran while one was open for 31% -> 33% of each run, Pallas kernels for 0% -> 0%
where the time goes in v1:
time: 258 us; the launch traced here: 256 us
  waiting for transfers between devices  89.5 us (35%)
  matrix products  54.3 us (21%)
  local copies, waits for them, and re-layouts  39.3 us (15%)
  blocking collectives  27.6 us (11%)
  starting transfers between devices  19.5 us (8%)
  between operations  14 us (5%)
  other arithmetic  11.9 us (5%)
    all_gather x1, waiting for transfers between devices, shards(): lax.all_gather(w_query, 'seq', axis=0, tiled=True)  45.4 us
    all_gather x1, waiting for transfers between devices, shards(): piece = lax.all_gather(stacked, 'seq', axis=0, tiled=True)  33.3 us
    dot_general x16, matrix products, one_head(): lax.dot_general(query_head, key_rows, (((1,), (1,)), ((), ())), preferred...  30 us
    all_gather x1, blocking collectives, shards(): lax.all_gather(w_key, 'seq', axis=0, tiled=True)  27.6 us
    dynamic_update_slice x32, local copies, waits for them, and re-layouts, attend_block(): result = lax.map(one_head, per_head)  12.5 us
    ppermute x3, starting transfers between devices, shifted(): return lax.ppermute(array, axis, pairs)  10.7 us
    ppermute x3, waiting for transfers between devices, shifted(): return lax.ppermute(array, axis, pairs)  9.39 us
    all_gather x1, local copies, waits for them, and re-layouts, shards(): piece = lax.all_gather(stacked, 'seq', axis=0, tiled=True)  8.62 us
  transfers between devices with their start and end apart: 7, of which 5 were waited for; matrix products, arithmetic and copies ran while one was open for 33% of the time, Pallas kernels for 0%

profile of v1, /device:TPU:1, one launch (start us, length us, event | category | flops | bytes accessed | tf_op | source)
XLA Modules:
  0.0 256.3 jit_solution(11627310281379975193)
XLA Ops:
  7.2 1.7 stack.2
  8.9 8.6 %all-to-all-start = ((bf16[32,64,128]{2,1,0:T(8,128)(2,1)}), bf16[32,64,128]{2,1,0:T(8,128)(2,1)S(1)}, u32[]{:S(2)}, u32[]{:S(2)}) async-start(bf16[32,64,128]{2,1,0:T(8,128)(2,1)} %stack.2), calls=%async_computation | async-start | bytes 1048576 | tf_op jit(solution)/shard_map/all_to_all | solution.py:66
  18.0 27.6 %all_gather.13 = bf16[2048,128]{1,0:T(8,128)(2,1)S(1)} all-gather(bf16[64,128]{1,0:T(8,128)(2,1)S(1)} %copy-done.3), channel_id=1, replica_groups=mesh['seq'=32,'grp'=8] {'seq'}, dimensions={0}, use_global_device_ids=true | all-gather | bytes 540672 | tf_op jit(solution)/shard_map/all_gather | solution.py:64
  45.6 0.7 convolution_convert_fusion.2
  46.4 0.7 convolution_convert_fusion.1
  47.1 0.7 pad_maximum_fusion
  47.9 0.7 all-gather.4.cloned.1.call-update
  48.6 0.7 all-gather.6.cloned.1.call-update
  50.2 1.9 fusion.23
  52.1 1.9 collective-permute-start
  54.1 2.8 %collective-permute-done = bf16[384,256]{0,1:T(8,128)(2,1)S(1)} collective-permute-done((bf16[384,256]{0,1:T(8,128)(2,1)}, bf16[384,256]{0,1:T(8,128)(2,1)S(1)}, u32[]{:S(2)}, u32[]{:S(2)}) %collective-permute-start) | collective-permute-done | bytes 196640 | tf_op jit(solution)/shard_map/ppermute | solution.py:15
  56.9 4.3 %collective-permute-start.1 = (bf16[384,256]{0,1:T(8,128)(2,1)S(1)}, bf16[384,256]{0,1:T(8,128)(2,1)S(1)}, u32[]{:S(2)}, u32[]{:S(2)}) collective-permute-start(bf16[384,256]{0,1:T(8,128)(2,1)S(1)} %collective-permute-done), channel_id=1, source_target_pairs={{0,8},{8,16},{16,24},{24,32},{32,40},{40,48},{48,56},{56,64},{64,7... | collective-permute-start | bytes 589832 | tf_op jit(solution)/shard_map/ppermute | solution.py:15
  61.2 3.1 %collective-permute-done.1 = bf16[384,256]{0,1:T(8,128)(2,1)S(1)} collective-permute-done((bf16[384,256]{0,1:T(8,128)(2,1)S(1)}, bf16[384,256]{0,1:T(8,128)(2,1)S(1)}, u32[]{:S(2)}, u32[]{:S(2)}) %collective-permute-start.1) | collective-permute-done | bytes 196640 | tf_op jit(solution)/shard_map/ppermute | solution.py:15
  64.3 4.6 %collective-permute-start.2 = (bf16[384,256]{0,1:T(8,128)(2,1)S(1)}, bf16[384,256]{0,1:T(8,128)(2,1)S(1)}, u32[]{:S(2)}, u32[]{:S(2)}) collective-permute-start(bf16[384,256]{0,1:T(8,128)(2,1)S(1)} %collective-permute-done.1), channel_id=1, source_target_pairs={{0,8},{8,16},{16,24},{24,32},{32,40},{40,48},{48,56},{56,64},{64,7... | collective-permute-start | bytes 589832 | tf_op jit(solution)/shard_map/ppermute | solution.py:15
  68.9 3.5 %collective-permute-done.2 = bf16[384,256]{0,1:T(8,128)(2,1)S(1)} collective-permute-done((bf16[384,256]{0,1:T(8,128)(2,1)S(1)}, bf16[384,256]{0,1:T(8,128)(2,1)S(1)}, u32[]{:S(2)}, u32[]{:S(2)}) %collective-permute-start.2) | collective-permute-done | bytes 196640 | tf_op jit(solution)/shard_map/ppermute | solution.py:15
  72.5 0.9 copy.20
  73.4 0.9 copy.21
  74.4 33.3 %all-gather.8.cloned.1.call-done = bf16[12288,256]{0,1:T(8,128)(2,1)} async-done(((bf16[384,256]{0,1:T(8,128)(2,1)}), bf16[12288,256]{0,1:T(8,128)(2,1)}) %all-gather.8.cloned.1.call-update) | async-done | bytes 6291472 | tf_op jit(solution)/shard_map/all_gather | solution.py:123
  107.7 8.6 %copy.23 = bf16[12288,256]{1,0:T(8,128)(2,1)} copy(bf16[12288,256]{0,1:T(8,128)(2,1)} %all-gather.8.cloned.1.call-done) | data formatting | bytes 12582912 | tf_op jit(solution)/shard_map/all_gather | solution.py:123
  116.3 5.3 %gather_fusion = bf16[384,256]{1,0:T(8,128)(2,1)S(1)} fusion(bf16[12288,256]{1,0:T(8,128)(2,1)} %copy.23, s32[1024]{0:T(1024)S(1)} %pad_clamp_fusion), kind=kCustom, calls=%fused_computation | custom fusion | bytes 394752 | tf_op jit(solution)/shard_map/jit(_take)/gather | solution.py:125
  121.5 0.8 select_select_fusion
  122.4 45.4 %all-gather.4.cloned.1.call-done = bf16[2048,2048]{1,0:T(8,128)(2,1)} async-done(((bf16[64,2048]{1,0:T(8,128)(2,1)}), bf16[2048,2048]{1,0:T(8,128)(2,1)}) %all-gather.4.cloned.1.call-update) | async-done | bytes 8388624 | tf_op jit(solution)/shard_map/all_gather | solution.py:63
  167.8 6.8 %fusion.12 = bf16[48,16,8,128]{3,2,1,0:T(8,128)(2,1)S(1)} fusion(bf16[2048,2048]{1,0:T(8,128)(2,1)} %all-gather.4.cloned.1.call-done, bf16[384,2048]{1,0:T(8,128)(2,1)S(1)} %copy-done, f32[2048]{0:T(1024)S(1)} %convert_element_type.32, f32[384]{0:T(512)S(1)} %add_rsqrt_fusion), kind=kOutput, calls=%fused_computation.22 | convolution fusion | flops 3225157632 | bytes 11544064 | tf_op jit(solution)/shard_map/dot_general | solution.py:71
  175.1 66.2 %while.12 = (s32[]{:T(128)}, bf16[16,384,128]{1,2,0:T(8,128)(2,1)}, bf16[16,384,128]{2,1,0:T(8,128)(2,1)S(1)}, bf16[1536,128]{1,0:T(8,128)(2,1)}, bf16[1536,128]...) while((s32[]{:T(128)}, bf16[16,384,128]{1,2,0:T(8,128)(2,1)}, ...), condition=%wide.region_4.5_spmd.clone, body=%wide.region_1.4_spmd.clone.sunk | while | flops 309165312 | bytes 10055833 | solution.py:52
  175.1 1.9 fusion.47
  178.6 0.7 constant_dynamic-update-slice_fusion.2
  179.2 1.9 fusion.47
  182.7 0.7 constant_dynamic-update-slice_fusion.2
  183.4 1.9 fusion.47
  186.9 0.7 constant_dynamic-update-slice_fusion.2
  187.5 1.9 fusion.47
  191.6 1.9 fusion.47
  195.8 1.9 fusion.47
  199.2 0.7 constant_dynamic-update-slice_fusion.2
  199.9 1.9 fusion.47
  203.4 0.7 constant_dynamic-update-slice_fusion.2
  204.0 1.9 fusion.47
  208.2 1.9 fusion.47
  212.3 1.9 fusion.47
  215.8 0.7 constant_dynamic-update-slice_fusion.2
  216.4 1.9 fusion.47
  220.6 1.9 fusion.47
  224.8 1.9 fusion.47
  229.0 1.9 fusion.47
  233.1 1.9 fusion.47
  236.5 0.7 constant_dynamic-update-slice_fusion.2
  237.2 1.9 fusion.47
  241.3 8.5 %fusion.11 = bf16[384,2048]{1,0:T(8,128)(2,1)} fusion(bf16[384,2048]{1,0:T(8,128)(2,1)S(1)} %copy-done, bf16[384,2048]{0,1:T(8,128)(2,1)} %bitcast.64, bf16[2048,2048]{1,0:T(8,128)(2,1)} %all-gather.6.cloned.1.call-done), kind=kOutput, calls=%fused_computation.19 | convolution fusion | flops 3223584768 | bytes 13107200 | tf_op jit(solution)/shard_map/dot_general | solution.py:103
  (122 shorter events, 33.4 us)
Async XLA Ops:
  7.2 10.4 %copy-start = (bf16[384,2048]{1,0:T(8,128)(2,1)S(1)}, bf16[384,2048]{1,0:T(8,128)(2,1)}, u32[]{:S(2)}) copy-start(bf16[384,2048]{1,0:T(8,128)(2,1)} %param.12) | copy-start | bytes 4718596
  7.2 10.8 %copy-start.3 = (bf16[64,128]{1,0:T(8,128)(2,1)S(1)}, bf16[64,128]{1,0:T(8,128)(2,1)}, u32[]{:S(2)}) copy-start(bf16[64,128]{1,0:T(8,128)(2,1)} %param.15) | copy-start | bytes 49156
  7.2 38.4 %copy-start.4 = (bf16[2048]{0:T(1024)(128)(2,1)S(1)}, bf16[2048]{0:T(1024)(128)(2,1)}, u32[]{:S(2)}) copy-start(bf16[2048]{0:T(1024)(128)(2,1)} %param.13) | copy-start | bytes 12292
  8.9 37.4 %all-to-all-start = ((bf16[32,64,128]{2,1,0:T(8,128)(2,1)}), bf16[32,64,128]{2,1,0:T(8,128)(2,1)S(1)}, u32[]{:S(2)}, u32[]{:S(2)}) async-start(bf16[32,64,128]{2,1,0:T(8,128)(2,1)} %stack.2), calls=%async_computation | async-start | bytes 1048576 | tf_op jit(solution)/shard_map/all_to_all | solution.py:66
  17.5 90.1 %all-gather.8.cloned.1.call-start = ((), (), s32[]{:S(2)}) async-start(), calls=%async_computation.3 | async-start | bytes 6488064 | tf_op jit(solution)/shard_map/all_gather | solution.py:123
  46.4 3.0 %copy-start.5 = (s32[96]{0:T(128)S(1)}, s32[96]{0:T(128)}, u32[]{:S(2)}) copy-start(s32[96]{0:T(128)} %param.19) | copy-start | bytes 1156
  46.4 3.8 %copy-start.2 = (s32[12288]{0:T(1024)S(1)}, s32[12288]{0:T(1024)}, u32[]{:S(2)}) copy-start(s32[12288]{0:T(1024)} %param.18) | copy-start | bytes 147460
  47.8 120.0 %all-gather.4.cloned.1.call-start = ((), (), s32[]{:S(2)}) async-start(), calls=%async_computation.1 | async-start | bytes 8650752 | tf_op jit(solution)/shard_map/all_gather | solution.py:63
  48.6 192.7 %all-gather.6.cloned.1.call-start = ((), (), s32[]{:S(2)}) async-start(), calls=%async_computation.2 | async-start | bytes 8650752 | tf_op jit(solution)/shard_map/all_gather | solution.py:105
  52.1 4.8 %collective-permute-start = (bf16[384,256]{0,1:T(8,128)(2,1)}, bf16[384,256]{0,1:T(8,128)(2,1)S(1)}, u32[]{:S(2)}, u32[]{:S(2)}) collective-permute-start(bf16[384,256]{0,1:T(8,128)(2,1)} %pad_maximum_fusion), channel_id=1, source_target_pairs={{0,8},{8,16},{16,24},{24,32},{32,40},{40,48},{48,56},{56,64},{64,7... | collective-permute-start | bytes 589832 | tf_op jit(solution)/shard_map/ppermute | solution.py:15
  56.9 7.4 %collective-permute-start.1 = (bf16[384,256]{0,1:T(8,128)(2,1)S(1)}, bf16[384,256]{0,1:T(8,128)(2,1)S(1)}, u32[]{:S(2)}, u32[]{:S(2)}) collective-permute-start(bf16[384,256]{0,1:T(8,128)(2,1)S(1)} %collective-permute-done), channel_id=1, source_target_pairs={{0,8},{8,16},{16,24},{24,32},{32,40},{40,48},{48,56},{56,64},{64,7... | collective-permute-start | bytes 589832 | tf_op jit(solution)/shard_map/ppermute | solution.py:15
  64.3 8.1 %collective-permute-start.2 = (bf16[384,256]{0,1:T(8,128)(2,1)S(1)}, bf16[384,256]{0,1:T(8,128)(2,1)S(1)}, u32[]{:S(2)}, u32[]{:S(2)}) collective-permute-start(bf16[384,256]{0,1:T(8,128)(2,1)S(1)} %collective-permute-done.1), channel_id=1, source_target_pairs={{0,8},{8,16},{16,24},{24,32},{32,40},{40,48},{48,56},{56,64},{64,7... | collective-permute-start | bytes 589832 | tf_op jit(solution)/shard_map/ppermute | solution.py:15
  177.0 1.0 copy-start.1
  181.1 1.0 copy-start.1
  185.3 1.0 copy-start.1
  189.4 1.0 copy-start.1
  193.5 1.0 copy-start.1
  197.6 1.0 copy-start.1
  201.7 1.0 copy-start.1
  205.9 1.0 copy-start.1
  210.0 1.0 copy-start.1
  214.2 1.0 copy-start.1
  218.3 1.0 copy-start.1
  222.5 1.0 copy-start.1
  226.7 1.0 copy-start.1
  230.8 1.0 copy-start.1
  234.9 1.0 copy-start.1
  239.1 1.0 copy-start.1
Sparse Core Ops, SparseCore 0:
  48.0 59.6 all-gather.7
  110.2 57.5 all-gather.3
  170.4 57.5 all-gather.5
